TPU v7x, 32 devices: a whole 2x2x4 slice. The times are simulated.
32 devices in a mesh: ord: 8 (over z, core), gx: 2 (over x), gy: 2 (over y).
Axes of the slice: x: 2, y: 2, z: 4, core: 2. Of those that a mesh axis runs over, the one named last changes fastest.
Arguments:
- distribution: float32 [256, 64, 8, 128], P('ord', 'gx', 'gy'), may hold values from -4.5 to 4.5
- relaxation: float32 [64, 8, 128], P('gx', 'gy'), may hold values from 0.05 to 5
Outputs:
- updated: float32 [256, 64, 8, 128], P('ord', 'gx', 'gy')
- temperature: float32 [64, 8, 128], P('gx', 'gy')
All inputs are finite; a program needn't handle non-finite values.
Results may differ from a plain program's by a relative error of at most 0.0003.
Values sent between devices are 32-bit elements; how exact they have to be, the bound alone decides.
A program may use at most 64 MiB of HBM per device.

v0:
```python
import jax
import jax.numpy as jnp
from jax import lax
from jax.sharding import PartitionSpec as P

NORD = 256
STEPS = 2
SWEEPS = 3
time_step = 0.4
limiter_eps = 0.01
diffusion_mass = 0.5
flux_weight = 2.0
golden_turn = 2.399963229728653


def extended(cells, sides, width):
    for axis, dim in sides:
        count = lax.axis_size(axis)
        ends = count - 1
        head = lax.slice_in_dim(cells, 0, width, axis=dim)
        tail = lax.slice_in_dim(cells, cells.shape[dim] - width, cells.shape[dim], axis=dim)
        cells = jnp.concatenate(
            [
                lax.ppermute(tail, axis, [(i, (i + 1) % count) for i in range(ends)]),
                cells,
                lax.ppermute(head, axis, [((i + 1) % count, i) for i in range(ends)]),
            ],
            axis=dim,
        )
    return cells


def directions(offset, length):
    ordinal = (offset + jnp.arange(length, dtype=jnp.int32)).astype(jnp.float32)
    height = 1.0 - (2.0 * ordinal + 1.0) / NORD
    radius = jnp.sqrt(1.0 - height * height)
    turned = golden_turn * ordinal
    return jnp.stack([radius * jnp.cos(turned), radius * jnp.sin(turned), height])


def window(values, anchor, length, axis_dim):
    return lax.slice_in_dim(values, anchor, anchor + length, axis=axis_dim)


def pad_along(values, width, axis_dim):
    widths = [
        (width, width) if dimension == axis_dim else (0, 0) for dimension in range(values.ndim)
    ]
    return jnp.pad(values, widths)


def source_of(current, local_temp, relax):
    return ((2.0 * relax - time_step) * current + 2.0 * time_step * local_temp) / (
        2.0 * relax + time_step
    )


def axis_flux(padded, temp_pad, relax_pad, along_speed, axis_dim):
    length = padded.shape[axis_dim] - 4
    lower_diff = window(padded, 1, length + 2, axis_dim) - window(padded, 0, length + 2, axis_dim)
    upper_diff = window(padded, 2, length + 2, axis_dim) - window(padded, 1, length + 2, axis_dim)
    centre = window(padded, 1, length + 2, axis_dim)
    slopes = (
        lower_diff * (upper_diff * upper_diff + limiter_eps)
        + upper_diff * (lower_diff * lower_diff + limiter_eps)
    ) / (lower_diff * lower_diff + upper_diff * upper_diff + 2.0 * limiter_eps)
    upwind_low = window(centre, 0, length + 1, axis_dim) + 0.5 * (
        1.0 - time_step * along_speed
    ) * window(slopes, 0, length + 1, axis_dim)
    upwind_high = window(centre, 1, length + 1, axis_dim) - 0.5 * (
        1.0 + time_step * along_speed
    ) * window(slopes, 1, length + 1, axis_dim)
    upwind = jnp.where(along_speed >= 0.0, upwind_low, upwind_high)
    temp_face = 0.5 * (
        window(temp_pad, 0, length + 1, axis_dim) + window(temp_pad, 1, length + 1, axis_dim)
    )
    relax_face = 0.5 * (
        window(relax_pad, 0, length + 1, axis_dim) + window(relax_pad, 1, length + 1, axis_dim)
    )
    edges = (2.0 * relax_face * upwind + 0.5 * time_step * temp_face) / (
        2.0 * relax_face + 0.5 * time_step
    )
    return along_speed * (window(edges, 1, length, axis_dim) - window(edges, 0, length, axis_dim))


def spread(flux_x_pad, flux_y_pad, flux_z):
    flux_z_pad = jnp.pad(flux_z, ((0, 0), (0, 0), (1, 1)))
    result = 0.5 * (flux_x_pad[2:, 1:-1, 1:-1] - flux_x_pad[:-2, 1:-1, 1:-1])
    result = result + 0.5 * (flux_y_pad[1:-1, 2:, 1:-1] - flux_y_pad[1:-1, :-2, 1:-1])
    return result + 0.5 * (flux_z_pad[:, :, 2:] - flux_z_pad[:, :, :-2])


def relax_sweep(potential_pad, driver):
    conduct = 1.0 / (1.0 + potential_pad * potential_pad)
    centre = conduct[1:-1, 1:-1, 1:-1]
    weighted = diffusion_mass * driver
    weights = diffusion_mass + jnp.zeros_like(driver)
    for axis_dim in range(3):
        for anchor in (0, 2):
            picker = tuple(
                (
                    (
                        slice(anchor, anchor + potential_pad.shape[axis_dim] - 2)
                        if dimension == axis_dim
                        else slice(1, -1)
                    )
                    for dimension in range(3)
                )
            )
            couple = 0.5 * (centre + conduct[picker])
            weighted = weighted + couple * potential_pad[picker]
            weights = weights + couple
    return weighted / weights


def transport(current, local_temp, relax, speeds):
    source = source_of(current, local_temp, relax)
    ordinal_rows = source.shape[0]
    stacked = jnp.concatenate([source, local_temp[None], relax[None]], 0)
    widened = extended(stacked, (("gx", 1), ("gy", 2)), 2)
    along_x = widened[:, :, 2:-2, :]
    along_y = widened[:, 2:-2, :, :]
    fluxes = axis_flux(
        along_x[:ordinal_rows],
        along_x[ordinal_rows : ordinal_rows + 1, 1:-1],
        along_x[ordinal_rows + 1 :, 1:-1],
        speeds[0][:, None, None, None],
        1,
    )
    fluxes = fluxes + axis_flux(
        along_y[:ordinal_rows],
        along_y[ordinal_rows : ordinal_rows + 1, :, 1:-1],
        along_y[ordinal_rows + 1 :, :, 1:-1],
        speeds[1][:, None, None, None],
        2,
    )
    fluxes = fluxes + axis_flux(
        pad_along(source, 2, 3),
        pad_along(local_temp[None], 1, 3),
        pad_along(relax[None], 1, 3),
        speeds[2][:, None, None, None],
        3,
    )
    return source - time_step * fluxes


def block_extend(stacked):
    widened = extended(stacked, (("gx", 1), ("gy", 2)), 1)
    return jnp.pad(widened, ((0, 0), (0, 0), (0, 0), (1, 1)))


def diffuse(shares, extend):
    energy = shares[0]
    widened = extend(shares[:3])
    driver = energy - flux_weight * spread(widened[1], widened[2], shares[3])
    potential = relax_sweep(widened[0], driver)
    for rounds in range(1, SWEEPS):
        potential = relax_sweep(extend(potential[None])[0], driver)
    return potential


def local(distribution, relaxation):
    local_count = distribution.shape[0]
    speeds = directions(lax.axis_index("ord") * local_count, local_count)
    current = distribution
    for repeat in range(STEPS):
        local_temp = lax.psum(jnp.sum(current, 0) / NORD, "ord")
        current = transport(current, local_temp, relaxation, speeds)
    partial_value = (
        jnp.concatenate(
            [jnp.sum(current, 0)[None], jnp.sum(speeds[:, :, None, None, None] * current[None], 1)],
            0,
        )
        / NORD
    )
    shares = lax.psum(partial_value, "ord")
    potential = diffuse(shares, block_extend)
    updated = source_of(current, potential, relaxation)
    return (updated, potential)


def solution(mesh):
    placed = (P("ord", "gx", "gy", None), P("gx", "gy", None))
    return jax.shard_map(
        local,
        mesh=mesh,
        in_specs=placed,
        out_specs=(P("ord", "gx", "gy", None), P("gx", "gy", None)),
        check_vma=False,
    )
```

profile of v0, /device:TPU:0, one launch (start us, length us, event | category | flops | bytes accessed | tf_op | source)
XLA Modules:
  0.0 365.7 jit_solution(15019233585724942882)
XLA Ops:
  7.2 2.0 reduce_sum.36
  12.2 56.1 %all-reduce.13.cloned.1.call-done = f32[32,4,128]{2,1,0:T(4,128)} async-done(((f32[32,4,128]{2,1,0:T(4,128)}), f32[32,4,128]{2,1,0:T(4,128)}) %all-reduce.13.cloned.1.call-update) | async-done | bytes 65552 | tf_op jit(solution)/shard_map/psum | solution.py:167
  71.5 2.4 add_divide_fusion.1
  74.3 3.4 collective-permute-start
  79.0 2.6 fusion.4
  81.5 3.0 collective-permute-done.1
  85.2 3.5 collective-permute-start.2
  93.6 21.6 %collective-permute-done.2 = f32[34,36,2,128]{3,1,2,0:T(8,128)S(1)} collective-permute-done((f32[34,36,2,128]{3,1,2,0:T(8,128)S(1)}, f32[34,36,2,128]{3,1,2,0:T(8,128)S(1)}, u32[]{:S(2)}, u32[]{:S(2)}) %collective-permute-start.2) | collective-permute-done | bytes 1253408 | tf_op jit(solution)/shard_map/ppermute | solution.py:24
  115.3 4.2 %collective-permute-done.3 = f32[34,36,2,128]{3,1,2,0:T(8,128)S(1)} collective-permute-done((f32[34,36,2,128]{3,1,2,0:T(8,128)S(1)}, f32[34,36,2,128]{3,1,2,0:T(8,128)S(1)}, u32[]{:S(2)}, u32[]{:S(2)}) %collective-permute-start.3) | collective-permute-done | bytes 1253408 | tf_op jit(solution)/shard_map/ppermute | solution.py:26
  119.5 3.6 fusion.18
  123.1 3.5 add_divide_fusion.3
  131.0 53.0 %all-reduce.15.cloned.1.call-done = f32[32,4,128]{2,1,0:T(4,128)} async-done(((f32[32,4,128]{2,1,0:T(4,128)}), f32[32,4,128]{2,1,0:T(4,128)}) %all-reduce.15.cloned.1.call-update) | async-done | bytes 65552 | tf_op jit(solution)/shard_map/psum | solution.py:167
  187.1 2.4 add_divide_fusion
  189.8 3.4 collective-permute-start.4
  194.8 2.6 fusion.12
  197.4 2.8 collective-permute-done.5
  200.8 3.5 collective-permute-start.6
  209.1 21.8 %collective-permute-done.6 = f32[34,36,2,128]{3,1,2,0:T(8,128)S(1)} collective-permute-done((f32[34,36,2,128]{3,1,2,0:T(8,128)S(1)}, f32[34,36,2,128]{3,1,2,0:T(8,128)S(1)}, u32[]{:S(2)}, u32[]{:S(2)}) %collective-permute-start.6) | collective-permute-done | bytes 1253408 | tf_op jit(solution)/shard_map/ppermute | solution.py:24
  230.9 4.2 %collective-permute-done.7 = f32[34,36,2,128]{3,1,2,0:T(8,128)S(1)} collective-permute-done((f32[34,36,2,128]{3,1,2,0:T(8,128)S(1)}, f32[34,36,2,128]{3,1,2,0:T(8,128)S(1)}, u32[]{:S(2)}, u32[]{:S(2)}) %collective-permute-start.7) | collective-permute-done | bytes 1253408 | tf_op jit(solution)/shard_map/ppermute | solution.py:26
  235.1 3.6 fusion.21
  238.7 3.5 add_divide_fusion.2
  243.9 1.8 fusion.156
  248.7 53.9 %all-reduce.17.cloned.1.call-done = f32[4,32,4,128]{3,2,1,0:T(4,128)} async-done(((f32[4,32,4,128]{3,2,1,0:T(4,128)}), f32[4,32,4,128]{3,2,1,0:T(4,128)}) %all-reduce.17.cloned.1.call-update) | async-done | bytes 262160 | tf_op jit(solution)/shard_map/psum | solution.py:176
  303.2 3.4 collective-permute-start.8
  308.9 3.3 collective-permute-done.9
  312.2 3.4 collective-permute-start.10
  318.0 3.6 collective-permute-done.11
  327.1 4.2 %collective-permute-done.13 = f32[1,1,4,128]{3,2,1,0:T(4,128)S(1)} collective-permute-done((f32[1,1,4,128]{3,2,1,0:T(4,128)S(1)}, f32[1,1,4,128]{3,2,1,0:T(4,128)S(1)}, u32[]{:S(2)}, u32[]{:S(2)}) %collective-permute-start.13) | collective-permute-done | bytes 2080 | tf_op jit(solution)/shard_map/ppermute | solution.py:26
  334.3 4.2 %collective-permute-done.15 = f32[1,34,1,128]{3,2,1,0:T(1,128)S(1)} collective-permute-done((f32[1,34,1,128]{3,2,1,0:T(1,128)S(1)}, f32[1,34,1,128]{3,2,1,0:T(1,128)S(1)}, u32[]{:S(2)}, u32[]{:S(2)}) %collective-permute-start.15) | collective-permute-done | bytes 17440 | tf_op jit(solution)/shard_map/ppermute | solution.py:26
  342.6 4.2 %collective-permute-done.17 = f32[1,1,4,128]{3,2,1,0:T(4,128)S(1)} collective-permute-done((f32[1,1,4,128]{3,2,1,0:T(4,128)S(1)}, f32[1,1,4,128]{3,2,1,0:T(4,128)S(1)}, u32[]{:S(2)}, u32[]{:S(2)}) %collective-permute-start.17) | collective-permute-done | bytes 2080 | tf_op jit(solution)/shard_map/ppermute | solution.py:26
  349.8 4.2 %collective-permute-done.19 = f32[1,34,1,128]{3,2,1,0:T(1,128)S(1)} collective-permute-done((f32[1,34,1,128]{3,2,1,0:T(1,128)S(1)}, f32[1,34,1,128]{3,2,1,0:T(1,128)S(1)}, u32[]{:S(2)}, u32[]{:S(2)}) %collective-permute-start.19) | collective-permute-done | bytes 17440 | tf_op jit(solution)/shard_map/ppermute | solution.py:26
  356.1 3.1 copy.53
  (110 shorter events, 55.5 us)
Async XLA Ops:
  7.2 63.9 %copy-start = (f32[32,32,4,128]{3,2,1,0:T(4,128)S(1)}, f32[32,32,4,128]{3,2,1,0:T(4,128)}, u32[]{:S(2)}) copy-start(f32[32,32,4,128]{3,2,1,0:T(4,128)} %param.2) | copy-start | bytes 6291460
  7.2 61.1 %all-reduce.13.cloned.1.call-start = ((), (), s32[]{:S(2)}) async-start(), calls=%async_computation | async-start | bytes 131072 | tf_op jit(solution)/shard_map/psum | solution.py:167
  9.9 174.1 %all-reduce.15.cloned.1.call-start = ((), (), s32[]{:S(2)}) async-start(), calls=%async_computation.1 | async-start | bytes 131072 | tf_op jit(solution)/shard_map/psum | solution.py:167
  74.3 7.3 %collective-permute-start = (f32[34,2,4,128]{3,1,2,0:T(2,128)S(1)}, f32[34,2,4,128]{3,1,2,0:T(2,128)S(1)}, u32[]{:S(2)}, u32[]{:S(2)}) collective-permute-start(f32[34,2,4,128]{3,1,2,0:T(2,128)S(1)} %get-tuple-element.44), channel_id=1, source_target_pairs={{0,2},{1,3},{4,6},{5,7},{8,10},{9,11},{12,14},{13,15},{16,18},{17,... | collective-permute-start | bytes 417800 | tf_op jit(solution)/shard_map/ppermute | solution.py:24
  77.6 6.9 %collective-permute-start.1 = (f32[34,2,4,128]{3,1,2,0:T(2,128)S(1)}, f32[34,2,4,128]{3,1,2,0:T(2,128)S(1)}, u32[]{:S(2)}, u32[]{:S(2)}) collective-permute-start(f32[34,2,4,128]{3,1,2,0:T(2,128)S(1)} %get-tuple-element.45), channel_id=1, source_target_pairs={{2,0},{3,1},{6,4},{7,5},{10,8},{11,9},{14,12},{15,13},{18,16},{19,... | collective-permute-start | bytes 417800 | tf_op jit(solution)/shard_map/ppermute | solution.py:26
  85.2 30.0 %collective-permute-start.2 = (f32[34,36,2,128]{3,1,2,0:T(8,128)S(1)}, f32[34,36,2,128]{3,1,2,0:T(8,128)S(1)}, u32[]{:S(2)}, u32[]{:S(2)}) collective-permute-start(f32[34,36,2,128]{3,1,2,0:T(8,128)S(1)} %get-tuple-element.33), channel_id=1, source_target_pairs={{0,1},{2,3},{4,5},{6,7},{8,9},{10,11},{12,13},{14,15},{16,17},{18,... | collective-permute-start | bytes 3760136 | tf_op jit(solution)/shard_map/ppermute | solution.py:24
  88.7 30.7 %collective-permute-start.3 = (f32[34,36,2,128]{3,1,2,0:T(8,128)S(1)}, f32[34,36,2,128]{3,1,2,0:T(8,128)S(1)}, u32[]{:S(2)}, u32[]{:S(2)}) collective-permute-start(f32[34,36,2,128]{3,1,2,0:T(8,128)S(1)} %get-tuple-element.32), channel_id=1, source_target_pairs={{1,0},{3,2},{5,4},{7,6},{9,8},{11,10},{13,12},{15,14},{17,16},{19,... | collective-permute-start | bytes 3760136 | tf_op jit(solution)/shard_map/ppermute | solution.py:26
  126.6 1.8 copy-start.1
  130.9 171.6 %all-reduce.17.cloned.1.call-start = ((), (), s32[]{:S(2)}) async-start(), calls=%async_computation.2 | async-start | bytes 524288 | tf_op jit(solution)/shard_map/psum | solution.py:176
  189.8 7.5 %collective-permute-start.4 = (f32[34,2,4,128]{3,1,2,0:T(2,128)S(1)}, f32[34,2,4,128]{3,1,2,0:T(2,128)S(1)}, u32[]{:S(2)}, u32[]{:S(2)}) collective-permute-start(f32[34,2,4,128]{3,1,2,0:T(2,128)S(1)} %get-tuple-element.40), channel_id=1, source_target_pairs={{0,2},{1,3},{4,6},{5,7},{8,10},{9,11},{12,14},{13,15},{16,18},{17,... | collective-permute-start | bytes 417800 | tf_op jit(solution)/shard_map/ppermute | solution.py:24
  193.2 6.9 %collective-permute-start.5 = (f32[34,2,4,128]{3,1,2,0:T(2,128)S(1)}, f32[34,2,4,128]{3,1,2,0:T(2,128)S(1)}, u32[]{:S(2)}, u32[]{:S(2)}) collective-permute-start(f32[34,2,4,128]{3,1,2,0:T(2,128)S(1)} %get-tuple-element.41), channel_id=1, source_target_pairs={{2,0},{3,1},{6,4},{7,5},{10,8},{11,9},{14,12},{15,13},{18,16},{19,... | collective-permute-start | bytes 417800 | tf_op jit(solution)/shard_map/ppermute | solution.py:26
  200.8 30.0 %collective-permute-start.6 = (f32[34,36,2,128]{3,1,2,0:T(8,128)S(1)}, f32[34,36,2,128]{3,1,2,0:T(8,128)S(1)}, u32[]{:S(2)}, u32[]{:S(2)}) collective-permute-start(f32[34,36,2,128]{3,1,2,0:T(8,128)S(1)} %get-tuple-element.31), channel_id=1, source_target_pairs={{0,1},{2,3},{4,5},{6,7},{8,9},{10,11},{12,13},{14,15},{16,17},{18,... | collective-permute-start | bytes 3760136 | tf_op jit(solution)/shard_map/ppermute | solution.py:24
  204.3 30.7 %collective-permute-start.7 = (f32[34,36,2,128]{3,1,2,0:T(8,128)S(1)}, f32[34,36,2,128]{3,1,2,0:T(8,128)S(1)}, u32[]{:S(2)}, u32[]{:S(2)}) collective-permute-start(f32[34,36,2,128]{3,1,2,0:T(8,128)S(1)} %get-tuple-element.30), channel_id=1, source_target_pairs={{1,0},{3,2},{5,4},{7,6},{9,8},{11,10},{13,12},{15,14},{17,16},{19,... | collective-permute-start | bytes 3760136 | tf_op jit(solution)/shard_map/ppermute | solution.py:26
  245.8 1.3 copy-start.2
  303.2 5.6 %collective-permute-start.8 = (f32[3,1,4,128]{3,2,1,0:T(4,128)S(1)}, f32[3,1,4,128]{3,2,1,0:T(4,128)S(1)}, u32[]{:S(2)}, u32[]{:S(2)}) collective-permute-start(f32[3,1,4,128]{3,2,1,0:T(4,128)S(1)} %get-tuple-element.49), channel_id=1, source_target_pairs={{0,2},{1,3},{4,6},{5,7},{8,10},{9,11},{12,14},{13,15},{16,18},{17,... | collective-permute-start | bytes 18440 | tf_op jit(solution)/shard_map/ppermute | solution.py:24
  306.6 5.5 %collective-permute-start.9 = (f32[3,1,4,128]{3,2,1,0:T(4,128)S(1)}, f32[3,1,4,128]{3,2,1,0:T(4,128)S(1)}, u32[]{:S(2)}, u32[]{:S(2)}) collective-permute-start(f32[3,1,4,128]{3,2,1,0:T(4,128)S(1)} %get-tuple-element.50), channel_id=1, source_target_pairs={{2,0},{3,1},{6,4},{7,5},{10,8},{11,9},{14,12},{15,13},{18,16},{19,... | collective-permute-start | bytes 18440 | tf_op jit(solution)/shard_map/ppermute | solution.py:26
  312.2 5.8 %collective-permute-start.10 = (f32[3,34,1,128]{3,2,1,0:T(1,128)S(1)}, f32[3,34,1,128]{3,2,1,0:T(1,128)S(1)}, u32[]{:S(2)}, u32[]{:S(2)}) collective-permute-start(f32[3,34,1,128]{3,2,1,0:T(1,128)S(1)} %get-tuple-element.51), channel_id=1, source_target_pairs={{0,1},{2,3},{4,5},{6,7},{8,9},{10,11},{12,13},{14,15},{16,17},{18,... | collective-permute-start | bytes 156680 | tf_op jit(solution)/shard_map/ppermute | solution.py:24
  315.6 6.0 %collective-permute-start.11 = (f32[3,34,1,128]{3,2,1,0:T(1,128)S(1)}, f32[3,34,1,128]{3,2,1,0:T(1,128)S(1)}, u32[]{:S(2)}, u32[]{:S(2)}) collective-permute-start(f32[3,34,1,128]{3,2,1,0:T(1,128)S(1)} %get-tuple-element.52), channel_id=1, source_target_pairs={{1,0},{3,2},{5,4},{7,6},{9,8},{11,10},{13,12},{15,14},{17,16},{19,... | collective-permute-start | bytes 156680 | tf_op jit(solution)/shard_map/ppermute | solution.py:26
  322.5 33.3 %copy-start.3 = (f32[32,32,4,128]{3,1,2,0:T(8,128)S(1)}, f32[32,32,4,128]{3,1,2,0:T(8,128)}, u32[]{:S(2)}) copy-start(f32[32,32,4,128]{3,1,2,0:T(8,128)} %copy-done.2) | copy-start | bytes 6291460
  324.1 3.0 collective-permute-start.12
  325.8 5.5 %collective-permute-start.13 = (f32[1,1,4,128]{3,2,1,0:T(4,128)S(1)}, f32[1,1,4,128]{3,2,1,0:T(4,128)S(1)}, u32[]{:S(2)}, u32[]{:S(2)}) collective-permute-start(f32[1,1,4,128]{3,2,1,0:T(4,128)S(1)} %get-tuple-element.60), channel_id=1, source_target_pairs={{2,0},{3,1},{6,4},{7,5},{10,8},{11,9},{14,12},{15,13},{18,16},{19,... | collective-permute-start | bytes 6152 | tf_op jit(solution)/shard_map/ppermute | solution.py:26
  331.3 3.0 collective-permute-start.14
  332.9 5.6 %collective-permute-start.15 = (f32[1,34,1,128]{3,2,1,0:T(1,128)S(1)}, f32[1,34,1,128]{3,2,1,0:T(1,128)S(1)}, u32[]{:S(2)}, u32[]{:S(2)}) collective-permute-start(f32[1,34,1,128]{3,2,1,0:T(1,128)S(1)} %get-tuple-element.56), channel_id=1, source_target_pairs={{1,0},{3,2},{5,4},{7,6},{9,8},{11,10},{13,12},{15,14},{17,16},{19,... | collective-permute-start | bytes 52232 | tf_op jit(solution)/shard_map/ppermute | solution.py:26
  339.6 3.0 collective-permute-start.16
  341.2 5.5 %collective-permute-start.17 = (f32[1,1,4,128]{3,2,1,0:T(4,128)S(1)}, f32[1,1,4,128]{3,2,1,0:T(4,128)S(1)}, u32[]{:S(2)}, u32[]{:S(2)}) collective-permute-start(f32[1,1,4,128]{3,2,1,0:T(4,128)S(1)} %get-tuple-element.58), channel_id=1, source_target_pairs={{2,0},{3,1},{6,4},{7,5},{10,8},{11,9},{14,12},{15,13},{18,16},{19,... | collective-permute-start | bytes 6152 | tf_op jit(solution)/shard_map/ppermute | solution.py:26
  346.8 3.1 collective-permute-start.18
  348.4 5.6 %collective-permute-start.19 = (f32[1,34,1,128]{3,2,1,0:T(1,128)S(1)}, f32[1,34,1,128]{3,2,1,0:T(1,128)S(1)}, u32[]{:S(2)}, u32[]{:S(2)}) collective-permute-start(f32[1,34,1,128]{3,2,1,0:T(1,128)S(1)} %get-tuple-element.54), channel_id=1, source_target_pairs={{1,0},{3,2},{5,4},{7,6},{9,8},{11,10},{13,12},{15,14},{17,16},{19,... | collective-permute-start | bytes 52232 | tf_op jit(solution)/shard_map/ppermute | solution.py:26
Sparse Core Ops, SparseCore 0:
  10.9 57.4 all-reduce.12
  131.0 52.9 all-reduce.14
  248.8 53.7 all-reduce.16
where the time goes:
time: 367 us; the launch traced here: 366 us
  waiting for transfers between devices  245 us (67%)
  other arithmetic  55.6 us (15%)
  starting transfers between devices  40.7 us (11%)
  between operations  14.5 us (4%)
  local copies, waits for them, and re-layouts  10.4 us (3%)
    psum x2, waiting for transfers between devices, local(): local_temp = lax.psum(jnp.sum(current, 0) / NORD, 'ord')  109 us
    psum x1, waiting for transfers between devices, local(): shares = lax.psum(partial_value, 'ord')  53.9 us
    ppermute x10, waiting for transfers between devices, extended(): lax.ppermute(tail, axis, [(i, (i + 1) % count) for i in range(ends)])  43.7 us
    ppermute x10, waiting for transfers between devices, extended(): lax.ppermute(head, axis, [((i + 1) % count, i) for i in range(ends)])  37.9 us
    ppermute x10, starting transfers between devices, extended(): lax.ppermute(tail, axis, [(i, (i + 1) % count) for i in range(ends)])  27 us
    div x6, other arithmetic, axis_flux(): (lower_diff * (upper_diff * upper_diff + limiter_eps) + upper_diff * (low...  14.3 us
    ppermute x10, starting transfers between devices, extended(): lax.ppermute(head, axis, [((i + 1) % count, i) for i in range(ends)])  13.6 us
    div x6, other arithmetic, axis_flux(): (2.0 * relax_face * upwind + 0.5 * time_step * temp_face) / (2.0 * relax_...  11.4 us
  transfers between devices with their start and end apart: 23, of which 17 were waited for; matrix products, arithmetic and copies ran while one was open for 4% of the time, Pallas kernels for 0%

commit v1 on v0

--- a/solution.py
+++ b/solution.py
@@ -164,7 +164,9 @@
     speeds = directions(lax.axis_index("ord") * local_count, local_count)
     current = distribution
     for repeat in range(STEPS):
-        local_temp = lax.psum(jnp.sum(current, 0) / NORD, "ord")
+        block = jnp.sum(current, 0) / NORD
+        pieces = lax.all_gather(block, "ord")
+        local_temp = jnp.sum(pieces, axis=0)
         current = transport(current, local_temp, relaxation, speeds)
     partial_value = (
         jnp.concatenate(

time: 367 us -> 288 us (0.78)
  waiting for transfers between devices: 245 us -> 140 us
  blocking collectives: 0 us -> 31.5 us
    psum x2 -> x0, waiting for transfers between devices: 109 us -> none  [local(): local_temp = lax.psum(jnp.sum(current, 0) / NORD, 'ord')]
    all_gather x0 -> x2, blocking collectives: none -> 31.5 us  [local(): pieces = lax.all_gather(block, 'ord')]
    ppermute x10, waiting for transfers between devices: 43.7 us -> 49 us  [extended(): lax.ppermute(tail, axis, [(i, (i + 1) % count) for i in range(ends)])]
  transfers between devices with their start and end apart: 23 -> 21, of which waited for: 17 -> 15; matrix products, arithmetic and copies ran while one was open for 4% -> 6% of each run, Pallas kernels for 0% -> 0%
where the time goes in v1:
time: 288 us; the launch traced here: 287 us
  waiting for transfers between devices  140 us (49%)
  other arithmetic  52.4 us (18%)
  starting transfers between devices  39.5 us (14%)
  blocking collectives  31.5 us (11%)
  between operations  14.8 us (5%)
  local copies, waits for them, and re-layouts  8.67 us (3%)
    psum x1, waiting for transfers between devices, local(): shares = lax.psum(partial_value, 'ord')  54.8 us
    ppermute x10, waiting for transfers between devices, extended(): lax.ppermute(tail, axis, [(i, (i + 1) % count) for i in range(ends)])  49 us
    ppermute x10, waiting for transfers between devices, extended(): lax.ppermute(head, axis, [((i + 1) % count, i) for i in range(ends)])  36.1 us
    all_gather x2, blocking collectives, local(): pieces = lax.all_gather(block, 'ord')  31.5 us
    ppermute x10, starting transfers between devices, extended(): lax.ppermute(tail, axis, [(i, (i + 1) % count) for i in range(ends)])  25.8 us
    div x6, other arithmetic, axis_flux(): (lower_diff * (upper_diff * upper_diff + limiter_eps) + upper_diff * (low...  14.3 us
    ppermute x10, starting transfers between devices, extended(): lax.ppermute(head, axis, [((i + 1) % count, i) for i in range(ends)])  13.6 us
    div x6, other arithmetic, axis_flux(): (2.0 * relax_face * upwind + 0.5 * time_step * temp_face) / (2.0 * relax_...  11.4 us
  transfers between devices with their start and end apart: 21, of which 15 were waited for; matrix products, arithmetic and copies ran while one was open for 6% of the time, Pallas kernels for 0%

profile of v1, /device:TPU:0, one launch (start us, length us, event | category | flops | bytes accessed | tf_op | source)
XLA Modules:
  0.0 286.9 jit_solution(14693506546129851804)
XLA Ops:
  9.0 1.9 reduce_sum.58
  10.9 16.5 %all-gather = f32[256,4,128]{2,1,0:T(4,128)S(1)} all-gather(f32[32,4,128]{2,1,0:T(4,128)S(1)} %broadcast_multiply_fusion.3), channel_id=2, replica_groups=mesh['ord'=8,'gx'=2,'gy'=2] {'ord'}, dimensions={0}, use_global_device_ids=true | all-gather | bytes 589824 | tf_op jit(solution)/shard_map/all_gather | solution.py:168
  27.5 2.0 fusion.83
  29.9 3.4 %collective-permute-start = (f32[34,2,4,128]{3,1,2,0:T(2,128)S(1)}, f32[34,2,4,128]{3,1,2,0:T(2,128)S(1)}, u32[]{:S(2)}, u32[]{:S(2)}) collective-permute-start(f32[34,2,4,128]{3,1,2,0:T(2,128)S(1)} %get-tuple-element.44), channel_id=1, source_target_pairs={{0,2},{1,3},{4,6},{5,7},{8,10},{9,11},{12,14},{13,15},{16,18},{17,... | collective-permute-start | bytes 417800 | tf_op jit(solution)/shard_map/ppermute | solution.py:24
  34.9 2.4 add_divide_fusion.1
  37.6 2.5 fusion.4
  41.5 3.5 %collective-permute-start.2 = (f32[34,36,2,128]{3,1,2,0:T(8,128)S(1)}, f32[34,36,2,128]{3,1,2,0:T(8,128)S(1)}, u32[]{:S(2)}, u32[]{:S(2)}) collective-permute-start(f32[34,36,2,128]{3,1,2,0:T(8,128)S(1)} %get-tuple-element.33), channel_id=1, source_target_pairs={{0,1},{2,3},{4,5},{6,7},{8,9},{10,11},{12,13},{14,15},{16,17},{18,... | collective-permute-start | bytes 3760136 | tf_op jit(solution)/shard_map/ppermute | solution.py:24
  49.9 24.3 %collective-permute-done.2 = f32[34,36,2,128]{3,1,2,0:T(8,128)S(1)} collective-permute-done((f32[34,36,2,128]{3,1,2,0:T(8,128)S(1)}, f32[34,36,2,128]{3,1,2,0:T(8,128)S(1)}, u32[]{:S(2)}, u32[]{:S(2)}) %collective-permute-start.2) | collective-permute-done | bytes 1253408 | tf_op jit(solution)/shard_map/ppermute | solution.py:24
  74.3 4.2 %collective-permute-done.3 = f32[34,36,2,128]{3,1,2,0:T(8,128)S(1)} collective-permute-done((f32[34,36,2,128]{3,1,2,0:T(8,128)S(1)}, f32[34,36,2,128]{3,1,2,0:T(8,128)S(1)}, u32[]{:S(2)}, u32[]{:S(2)}) %collective-permute-start.3) | collective-permute-done | bytes 1253408 | tf_op jit(solution)/shard_map/ppermute | solution.py:26
  78.5 3.6 %fusion.18 = (f32[34,36,6,128]{3,1,2,0:T(8,128)S(1)}, f32[34,36,6,128]{3,1,2,0:T(8,128)S(1)}) fusion(f32[1,32,4,128]{3,1,2,0:T(8,128)S(1)} %bitcast.73, f32[34,36,2,128]{3,1,2,0:T(8,128)S(1)} %collective-permute-done.3, f32[34,2,4,128]{3,1,2,0:T(2,128)S(1)} %collective-permute-done.1, f32[1,32,4,128]{3,1,2,0:T(8,128)S(1)} %copy.46, ...), kind=kLoop, calls=%fused_computation.41 | loop fusion | flops 9400320 | bytes 12533760 | tf_op jit(solution)/shard_map/concatenate | solution.py:22
  82.1 3.5 %add_divide_fusion.3 = f32[32,32,6,128]{3,1,2,0:T(8,128)S(1)} fusion(f32[34,36,6,128]{3,1,2,0:T(8,128)S(1)} %get-tuple-element.37, f32[34,36,6,128]{3,1,2,0:T(8,128)S(1)} %get-tuple-element.36, f32[34,36,2,128]{3,1,2,0:T(8,128)S(1)} %collective-permute-done.3, f32[34,2,4,128]{3,1,2,0:T(2,128)S(1)} %collective-permute-done.1, ...), kind=kLoop, calls=%fused_computation.74 | loop fusion | flops 14155776 | bytes 14450688 | tf_op jit(solution)/shard_map/div | solution.py:63
  87.4 1.8 fusion.158
  89.3 15.0 %all-gather.1 = f32[256,4,128]{2,1,0:T(4,128)S(1)} all-gather(f32[32,4,128]{2,1,0:T(4,128)S(1)} %copy_multiply_fusion.1), channel_id=3, replica_groups=mesh['ord'=8,'gx'=2,'gy'=2] {'ord'}, dimensions={0}, use_global_device_ids=true | all-gather | bytes 589824 | tf_op jit(solution)/shard_map/all_gather | solution.py:168
  104.9 2.4 add_divide_fusion
  107.7 4.1 %collective-permute-start.4 = (f32[34,2,4,128]{3,1,2,0:T(2,128)S(1)}, f32[34,2,4,128]{3,1,2,0:T(2,128)S(1)}, u32[]{:S(2)}, u32[]{:S(2)}) collective-permute-start(f32[34,2,4,128]{3,1,2,0:T(2,128)S(1)} %get-tuple-element.40), channel_id=1, source_target_pairs={{0,2},{1,3},{4,6},{5,7},{8,10},{9,11},{12,14},{13,15},{16,18},{17,... | collective-permute-start | bytes 417800 | tf_op jit(solution)/shard_map/ppermute | solution.py:24
  113.4 2.6 fusion.12
  115.9 3.4 %collective-permute-done.5 = f32[34,2,4,128]{3,1,2,0:T(2,128)S(1)} collective-permute-done((f32[34,2,4,128]{3,1,2,0:T(2,128)S(1)}, f32[34,2,4,128]{3,1,2,0:T(2,128)S(1)}, u32[]{:S(2)}, u32[]{:S(2)}) %collective-permute-start.5) | collective-permute-done | bytes 139296 | tf_op jit(solution)/shard_map/ppermute | solution.py:26
  126.3 24.4 %collective-permute-done.6 = f32[34,36,2,128]{3,1,2,0:T(8,128)S(1)} collective-permute-done((f32[34,36,2,128]{3,1,2,0:T(8,128)S(1)}, f32[34,36,2,128]{3,1,2,0:T(8,128)S(1)}, u32[]{:S(2)}, u32[]{:S(2)}) %collective-permute-start.6) | collective-permute-done | bytes 1253408 | tf_op jit(solution)/shard_map/ppermute | solution.py:24
  150.7 4.2 %collective-permute-done.7 = f32[34,36,2,128]{3,1,2,0:T(8,128)S(1)} collective-permute-done((f32[34,36,2,128]{3,1,2,0:T(8,128)S(1)}, f32[34,36,2,128]{3,1,2,0:T(8,128)S(1)}, u32[]{:S(2)}, u32[]{:S(2)}) %collective-permute-start.7) | collective-permute-done | bytes 1253408 | tf_op jit(solution)/shard_map/ppermute | solution.py:26
  154.9 3.6 %fusion.21 = (f32[34,36,6,128]{3,1,2,0:T(8,128)S(1)}, f32[34,36,6,128]{3,1,2,0:T(8,128)S(1)}) fusion(f32[1,32,4,128]{3,1,2,0:T(8,128)S(1)} %bitcast.78, f32[34,36,2,128]{3,1,2,0:T(8,128)S(1)} %collective-permute-done.7, f32[34,2,4,128]{3,1,2,0:T(2,128)S(1)} %collective-permute-done.5, f32[1,32,4,128]{3,1,2,0:T(8,128)S(1)} %copy.50, ...), kind=kLoop, calls=%fused_computation.44 | loop fusion | flops 9400320 | bytes 12533760 | tf_op jit(solution)/shard_map/concatenate | solution.py:22
  158.6 3.5 %add_divide_fusion.2 = f32[32,32,6,128]{3,1,2,0:T(8,128)S(1)} fusion(f32[34,36,6,128]{3,1,2,0:T(8,128)S(1)} %get-tuple-element.35, f32[34,36,6,128]{3,1,2,0:T(8,128)S(1)} %get-tuple-element.34, f32[34,36,2,128]{3,1,2,0:T(8,128)S(1)} %collective-permute-done.7, f32[34,2,4,128]{3,1,2,0:T(2,128)S(1)} %collective-permute-done.5, ...), kind=kLoop, calls=%fused_computation.73 | loop fusion | flops 14155776 | bytes 14450688 | tf_op jit(solution)/shard_map/div | solution.py:63
  163.8 1.9 fusion.156
  168.6 54.8 %all-reduce.11.cloned.1.call-done = f32[4,32,4,128]{3,2,1,0:T(4,128)} async-done(((f32[4,32,4,128]{3,2,1,0:T(4,128)}), f32[4,32,4,128]{3,2,1,0:T(4,128)}) %all-reduce.11.cloned.1.call-update) | async-done | bytes 262160 | tf_op jit(solution)/shard_map/psum | solution.py:178
  224.1 3.4 %collective-permute-start.8 = (f32[3,1,4,128]{3,2,1,0:T(4,128)S(1)}, f32[3,1,4,128]{3,2,1,0:T(4,128)S(1)}, u32[]{:S(2)}, u32[]{:S(2)}) collective-permute-start(f32[3,1,4,128]{3,2,1,0:T(4,128)S(1)} %get-tuple-element.49), channel_id=1, source_target_pairs={{0,2},{1,3},{4,6},{5,7},{8,10},{9,11},{12,14},{13,15},{16,18},{17,... | collective-permute-start | bytes 18440 | tf_op jit(solution)/shard_map/ppermute | solution.py:24
  229.7 3.3 %collective-permute-done.9 = f32[3,1,4,128]{3,2,1,0:T(4,128)S(1)} collective-permute-done((f32[3,1,4,128]{3,2,1,0:T(4,128)S(1)}, f32[3,1,4,128]{3,2,1,0:T(4,128)S(1)}, u32[]{:S(2)}, u32[]{:S(2)}) %collective-permute-start.9) | collective-permute-done | bytes 6176 | tf_op jit(solution)/shard_map/ppermute | solution.py:26
  233.1 3.4 %collective-permute-start.10 = (f32[3,34,1,128]{3,2,1,0:T(1,128)S(1)}, f32[3,34,1,128]{3,2,1,0:T(1,128)S(1)}, u32[]{:S(2)}, u32[]{:S(2)}) collective-permute-start(f32[3,34,1,128]{3,2,1,0:T(1,128)S(1)} %get-tuple-element.51), channel_id=1, source_target_pairs={{0,1},{2,3},{4,5},{6,7},{8,9},{10,11},{12,13},{14,15},{16,17},{18,... | collective-permute-start | bytes 156680 | tf_op jit(solution)/shard_map/ppermute | solution.py:24
  238.9 3.6 %collective-permute-done.11 = f32[3,34,1,128]{3,2,1,0:T(1,128)S(1)} collective-permute-done((f32[3,34,1,128]{3,2,1,0:T(1,128)S(1)}, f32[3,34,1,128]{3,2,1,0:T(1,128)S(1)}, u32[]{:S(2)}, u32[]{:S(2)}) %collective-permute-start.11) | collective-permute-done | bytes 52256 | tf_op jit(solution)/shard_map/ppermute | solution.py:26
  247.9 4.2 %collective-permute-done.13 = f32[1,1,4,128]{3,2,1,0:T(4,128)S(1)} collective-permute-done((f32[1,1,4,128]{3,2,1,0:T(4,128)S(1)}, f32[1,1,4,128]{3,2,1,0:T(4,128)S(1)}, u32[]{:S(2)}, u32[]{:S(2)}) %collective-permute-start.13) | collective-permute-done | bytes 2080 | tf_op jit(solution)/shard_map/ppermute | solution.py:26
  255.2 4.2 %collective-permute-done.15 = f32[1,34,1,128]{3,2,1,0:T(1,128)S(1)} collective-permute-done((f32[1,34,1,128]{3,2,1,0:T(1,128)S(1)}, f32[1,34,1,128]{3,2,1,0:T(1,128)S(1)}, u32[]{:S(2)}, u32[]{:S(2)}) %collective-permute-start.15) | collective-permute-done | bytes 17440 | tf_op jit(solution)/shard_map/ppermute | solution.py:26
  263.4 4.2 %collective-permute-done.17 = f32[1,1,4,128]{3,2,1,0:T(4,128)S(1)} collective-permute-done((f32[1,1,4,128]{3,2,1,0:T(4,128)S(1)}, f32[1,1,4,128]{3,2,1,0:T(4,128)S(1)}, u32[]{:S(2)}, u32[]{:S(2)}) %collective-permute-start.17) | collective-permute-done | bytes 2080 | tf_op jit(solution)/shard_map/ppermute | solution.py:26
  270.7 4.2 %collective-permute-done.19 = f32[1,34,1,128]{3,2,1,0:T(1,128)S(1)} collective-permute-done((f32[1,34,1,128]{3,2,1,0:T(1,128)S(1)}, f32[1,34,1,128]{3,2,1,0:T(1,128)S(1)}, u32[]{:S(2)}, u32[]{:S(2)}) %collective-permute-start.19) | collective-permute-done | bytes 17440 | tf_op jit(solution)/shard_map/ppermute | solution.py:26
  276.9 3.1 %copy.55 = f32[32,32,4,128]{3,2,1,0:T(4,128)} copy(f32[32,32,4,128]{3,1,2,0:T(8,128)S(1)} %add_divide_fusion.6) | data formatting | bytes 4194304
  (106 shorter events, 49.2 us)
Async XLA Ops:
  7.2 216.2 %all-reduce.11.cloned.1.call-start = ((), (), s32[]{:S(2)}) async-start(), calls=%async_computation | async-start | bytes 524288 | tf_op jit(solution)/shard_map/psum | solution.py:178
  29.9 10.2 %collective-permute-start = (f32[34,2,4,128]{3,1,2,0:T(2,128)S(1)}, f32[34,2,4,128]{3,1,2,0:T(2,128)S(1)}, u32[]{:S(2)}, u32[]{:S(2)}) collective-permute-start(f32[34,2,4,128]{3,1,2,0:T(2,128)S(1)} %get-tuple-element.44), channel_id=1, source_target_pairs={{0,2},{1,3},{4,6},{5,7},{8,10},{9,11},{12,14},{13,15},{16,18},{17,... | collective-permute-start | bytes 417800 | tf_op jit(solution)/shard_map/ppermute | solution.py:24
  33.3 7.5 %collective-permute-start.1 = (f32[34,2,4,128]{3,1,2,0:T(2,128)S(1)}, f32[34,2,4,128]{3,1,2,0:T(2,128)S(1)}, u32[]{:S(2)}, u32[]{:S(2)}) collective-permute-start(f32[34,2,4,128]{3,1,2,0:T(2,128)S(1)} %get-tuple-element.45), channel_id=1, source_target_pairs={{2,0},{3,1},{6,4},{7,5},{10,8},{11,9},{14,12},{15,13},{18,16},{19,... | collective-permute-start | bytes 417800 | tf_op jit(solution)/shard_map/ppermute | solution.py:26
  41.5 32.7 %collective-permute-start.2 = (f32[34,36,2,128]{3,1,2,0:T(8,128)S(1)}, f32[34,36,2,128]{3,1,2,0:T(8,128)S(1)}, u32[]{:S(2)}, u32[]{:S(2)}) collective-permute-start(f32[34,36,2,128]{3,1,2,0:T(8,128)S(1)} %get-tuple-element.33), channel_id=1, source_target_pairs={{0,1},{2,3},{4,5},{6,7},{8,9},{10,11},{12,13},{14,15},{16,17},{18,... | collective-permute-start | bytes 3760136 | tf_op jit(solution)/shard_map/ppermute | solution.py:24
  45.0 33.4 %collective-permute-start.3 = (f32[34,36,2,128]{3,1,2,0:T(8,128)S(1)}, f32[34,36,2,128]{3,1,2,0:T(8,128)S(1)}, u32[]{:S(2)}, u32[]{:S(2)}) collective-permute-start(f32[34,36,2,128]{3,1,2,0:T(8,128)S(1)} %get-tuple-element.32), channel_id=1, source_target_pairs={{1,0},{3,2},{5,4},{7,6},{9,8},{11,10},{13,12},{15,14},{17,16},{19,... | collective-permute-start | bytes 3760136 | tf_op jit(solution)/shard_map/ppermute | solution.py:26
  85.6 1.8 copy-start
  107.7 8.2 %collective-permute-start.4 = (f32[34,2,4,128]{3,1,2,0:T(2,128)S(1)}, f32[34,2,4,128]{3,1,2,0:T(2,128)S(1)}, u32[]{:S(2)}, u32[]{:S(2)}) collective-permute-start(f32[34,2,4,128]{3,1,2,0:T(2,128)S(1)} %get-tuple-element.40), channel_id=1, source_target_pairs={{0,2},{1,3},{4,6},{5,7},{8,10},{9,11},{12,14},{13,15},{16,18},{17,... | collective-permute-start | bytes 417800 | tf_op jit(solution)/shard_map/ppermute | solution.py:24
  111.8 7.5 %collective-permute-start.5 = (f32[34,2,4,128]{3,1,2,0:T(2,128)S(1)}, f32[34,2,4,128]{3,1,2,0:T(2,128)S(1)}, u32[]{:S(2)}, u32[]{:S(2)}) collective-permute-start(f32[34,2,4,128]{3,1,2,0:T(2,128)S(1)} %get-tuple-element.41), channel_id=1, source_target_pairs={{2,0},{3,1},{6,4},{7,5},{10,8},{11,9},{14,12},{15,13},{18,16},{19,... | collective-permute-start | bytes 417800 | tf_op jit(solution)/shard_map/ppermute | solution.py:26
  120.0 30.7 %collective-permute-start.6 = (f32[34,36,2,128]{3,1,2,0:T(8,128)S(1)}, f32[34,36,2,128]{3,1,2,0:T(8,128)S(1)}, u32[]{:S(2)}, u32[]{:S(2)}) collective-permute-start(f32[34,36,2,128]{3,1,2,0:T(8,128)S(1)} %get-tuple-element.31), channel_id=1, source_target_pairs={{0,1},{2,3},{4,5},{6,7},{8,9},{10,11},{12,13},{14,15},{16,17},{18,... | collective-permute-start | bytes 3760136 | tf_op jit(solution)/shard_map/ppermute | solution.py:24
  121.6 33.4 %collective-permute-start.7 = (f32[34,36,2,128]{3,1,2,0:T(8,128)S(1)}, f32[34,36,2,128]{3,1,2,0:T(8,128)S(1)}, u32[]{:S(2)}, u32[]{:S(2)}) collective-permute-start(f32[34,36,2,128]{3,1,2,0:T(8,128)S(1)} %get-tuple-element.30), channel_id=1, source_target_pairs={{1,0},{3,2},{5,4},{7,6},{9,8},{11,10},{13,12},{15,14},{17,16},{19,... | collective-permute-start | bytes 3760136 | tf_op jit(solution)/shard_map/ppermute | solution.py:26
  165.7 1.3 copy-start.1
  224.1 5.6 %collective-permute-start.8 = (f32[3,1,4,128]{3,2,1,0:T(4,128)S(1)}, f32[3,1,4,128]{3,2,1,0:T(4,128)S(1)}, u32[]{:S(2)}, u32[]{:S(2)}) collective-permute-start(f32[3,1,4,128]{3,2,1,0:T(4,128)S(1)} %get-tuple-element.49), channel_id=1, source_target_pairs={{0,2},{1,3},{4,6},{5,7},{8,10},{9,11},{12,14},{13,15},{16,18},{17,... | collective-permute-start | bytes 18440 | tf_op jit(solution)/shard_map/ppermute | solution.py:24
  227.5 5.5 %collective-permute-start.9 = (f32[3,1,4,128]{3,2,1,0:T(4,128)S(1)}, f32[3,1,4,128]{3,2,1,0:T(4,128)S(1)}, u32[]{:S(2)}, u32[]{:S(2)}) collective-permute-start(f32[3,1,4,128]{3,2,1,0:T(4,128)S(1)} %get-tuple-element.50), channel_id=1, source_target_pairs={{2,0},{3,1},{6,4},{7,5},{10,8},{11,9},{14,12},{15,13},{18,16},{19,... | collective-permute-start | bytes 18440 | tf_op jit(solution)/shard_map/ppermute | solution.py:26
  233.1 5.8 %collective-permute-start.10 = (f32[3,34,1,128]{3,2,1,0:T(1,128)S(1)}, f32[3,34,1,128]{3,2,1,0:T(1,128)S(1)}, u32[]{:S(2)}, u32[]{:S(2)}) collective-permute-start(f32[3,34,1,128]{3,2,1,0:T(1,128)S(1)} %get-tuple-element.51), channel_id=1, source_target_pairs={{0,1},{2,3},{4,5},{6,7},{8,9},{10,11},{12,13},{14,15},{16,17},{18,... | collective-permute-start | bytes 156680 | tf_op jit(solution)/shard_map/ppermute | solution.py:24
  236.5 6.0 %collective-permute-start.11 = (f32[3,34,1,128]{3,2,1,0:T(1,128)S(1)}, f32[3,34,1,128]{3,2,1,0:T(1,128)S(1)}, u32[]{:S(2)}, u32[]{:S(2)}) collective-permute-start(f32[3,34,1,128]{3,2,1,0:T(1,128)S(1)} %get-tuple-element.52), channel_id=1, source_target_pairs={{1,0},{3,2},{5,4},{7,6},{9,8},{11,10},{13,12},{15,14},{17,16},{19,... | collective-permute-start | bytes 156680 | tf_op jit(solution)/shard_map/ppermute | solution.py:26
  243.3 33.3 %copy-start.2 = (f32[32,32,4,128]{3,1,2,0:T(8,128)S(1)}, f32[32,32,4,128]{3,1,2,0:T(8,128)}, u32[]{:S(2)}) copy-start(f32[32,32,4,128]{3,1,2,0:T(8,128)} %copy-done.1) | copy-start | bytes 6291460
  245.0 3.0 %collective-permute-start.12 = (f32[1,1,4,128]{3,2,1,0:T(4,128)S(1)}, f32[1,1,4,128]{3,2,1,0:T(4,128)S(1)}, u32[]{:S(2)}, u32[]{:S(2)}) collective-permute-start(f32[1,1,4,128]{3,2,1,0:T(4,128)S(1)} %get-tuple-element.59), channel_id=1, source_target_pairs={{0,2},{1,3},{4,6},{5,7},{8,10},{9,11},{12,14},{13,15},{16,18},{17,... | collective-permute-start | bytes 6152 | tf_op jit(solution)/shard_map/ppermute | solution.py:24
  246.6 5.5 %collective-permute-start.13 = (f32[1,1,4,128]{3,2,1,0:T(4,128)S(1)}, f32[1,1,4,128]{3,2,1,0:T(4,128)S(1)}, u32[]{:S(2)}, u32[]{:S(2)}) collective-permute-start(f32[1,1,4,128]{3,2,1,0:T(4,128)S(1)} %get-tuple-element.60), channel_id=1, source_target_pairs={{2,0},{3,1},{6,4},{7,5},{10,8},{11,9},{14,12},{15,13},{18,16},{19,... | collective-permute-start | bytes 6152 | tf_op jit(solution)/shard_map/ppermute | solution.py:26
  252.1 3.0 %collective-permute-start.14 = (f32[1,34,1,128]{3,2,1,0:T(1,128)S(1)}, f32[1,34,1,128]{3,2,1,0:T(1,128)S(1)}, u32[]{:S(2)}, u32[]{:S(2)}) collective-permute-start(f32[1,34,1,128]{3,2,1,0:T(1,128)S(1)} %get-tuple-element.55), channel_id=1, source_target_pairs={{0,1},{2,3},{4,5},{6,7},{8,9},{10,11},{12,13},{14,15},{16,17},{18,... | collective-permute-start | bytes 52232 | tf_op jit(solution)/shard_map/ppermute | solution.py:24
  253.7 5.6 %collective-permute-start.15 = (f32[1,34,1,128]{3,2,1,0:T(1,128)S(1)}, f32[1,34,1,128]{3,2,1,0:T(1,128)S(1)}, u32[]{:S(2)}, u32[]{:S(2)}) collective-permute-start(f32[1,34,1,128]{3,2,1,0:T(1,128)S(1)} %get-tuple-element.56), channel_id=1, source_target_pairs={{1,0},{3,2},{5,4},{7,6},{9,8},{11,10},{13,12},{15,14},{17,16},{19,... | collective-permute-start | bytes 52232 | tf_op jit(solution)/shard_map/ppermute | solution.py:26
  260.4 3.0 %collective-permute-start.16 = (f32[1,1,4,128]{3,2,1,0:T(4,128)S(1)}, f32[1,1,4,128]{3,2,1,0:T(4,128)S(1)}, u32[]{:S(2)}, u32[]{:S(2)}) collective-permute-start(f32[1,1,4,128]{3,2,1,0:T(4,128)S(1)} %get-tuple-element.57), channel_id=1, source_target_pairs={{0,2},{1,3},{4,6},{5,7},{8,10},{9,11},{12,14},{13,15},{16,18},{17,... | collective-permute-start | bytes 6152 | tf_op jit(solution)/shard_map/ppermute | solution.py:24
  262.1 5.5 %collective-permute-start.17 = (f32[1,1,4,128]{3,2,1,0:T(4,128)S(1)}, f32[1,1,4,128]{3,2,1,0:T(4,128)S(1)}, u32[]{:S(2)}, u32[]{:S(2)}) collective-permute-start(f32[1,1,4,128]{3,2,1,0:T(4,128)S(1)} %get-tuple-element.58), channel_id=1, source_target_pairs={{2,0},{3,1},{6,4},{7,5},{10,8},{11,9},{14,12},{15,13},{18,16},{19,... | collective-permute-start | bytes 6152 | tf_op jit(solution)/shard_map/ppermute | solution.py:26
  267.6 3.1 %collective-permute-start.18 = (f32[1,34,1,128]{3,2,1,0:T(1,128)S(1)}, f32[1,34,1,128]{3,2,1,0:T(1,128)S(1)}, u32[]{:S(2)}, u32[]{:S(2)}) collective-permute-start(f32[1,34,1,128]{3,2,1,0:T(1,128)S(1)} %get-tuple-element.53), channel_id=1, source_target_pairs={{0,1},{2,3},{4,5},{6,7},{8,9},{10,11},{12,13},{14,15},{16,17},{18,... | collective-permute-start | bytes 52232 | tf_op jit(solution)/shard_map/ppermute | solution.py:24
  269.2 5.6 %collective-permute-start.19 = (f32[1,34,1,128]{3,2,1,0:T(1,128)S(1)}, f32[1,34,1,128]{3,2,1,0:T(1,128)S(1)}, u32[]{:S(2)}, u32[]{:S(2)}) collective-permute-start(f32[1,34,1,128]{3,2,1,0:T(1,128)S(1)} %get-tuple-element.54), channel_id=1, source_target_pairs={{1,0},{3,2},{5,4},{7,6},{9,8},{11,10},{13,12},{15,14},{17,16},{19,... | collective-permute-start | bytes 52232 | tf_op jit(solution)/shard_map/ppermute | solution.py:26
Sparse Core Ops, SparseCore 0:
  168.7 54.6 all-reduce.10
